TPU v7x, 32 devices: a whole 2x2x4 slice. The times are simulated.
32 devices in a mesh: seq: 8 (over z, y), head: 4 (over x, core).
Axes of the slice: x: 2, y: 2, z: 4, core: 2. Of those that a mesh axis runs over, the one named last changes fastest.
Arguments:
- query: bfloat16 [8192, 4096], P('seq', 'head'), may hold values from -0.15625 to 0.15625
- key: bfloat16 [8192, 4096], P('seq', 'head'), may hold values from -0.15625 to 0.15625
- value: bfloat16 [8192, 4096], P('seq', 'head'), may hold values from -18 to 18, as said below
- level_coef: float32 [4, 32, 8192], P(None, 'head', 'seq'), may hold values from 0.25 to 2.5
- gain: float32 [4096], P('head'), may hold values from 0.5 to 1.5
- cotangent: bfloat16 [8192, 4096], P('seq', 'head'), may hold values from -0.625 to 0.625
Outputs:
- mixed: bfloat16 [8192, 4096], P('seq', 'head')
- grad_query: bfloat16 [8192, 4096], P('seq', 'head')
- grad_key: bfloat16 [8192, 4096], P('seq', 'head')
- grad_value: bfloat16 [8192, 4096], P('seq', 'head')
- grad_level: float32 [4, 32, 8192], P(None, 'head', 'seq')
- grad_gain: float32 [4096], P('head')
Inputs may be any that keep to these rules, and one draw needn't show every extreme that they name: `value`: real values.
All inputs are finite; a program needn't handle non-finite values.
Results may differ from a plain program's by a relative error of at most 0.0065.
Values sent between devices are 32-bit elements; how exact they have to be, the bound alone decides.
No kernel may reach another device: no remote copies, remote signals or barrier semaphores. Data moves between devices by JAX's collectives and lax.ppermute only.
A program may use at most 128 MiB of HBM per device.

v0:
```python
import jax
import jax.numpy as jnp
from jax import lax
from jax.sharding import PartitionSpec as P

HEADS = 32
HEAD_DIM = 128
EPS = 1e-06


def from_partner(block, axis, apart):
    count = lax.axis_size(axis)
    route = []
    for low in range(count):
        high = low | 1 << apart
        if high != low and high < count:
            route += [(low, high), (high, low)]
    return lax.ppermute(block, axis, route)


def body(query, key, value, level_coef, gain, cotangent):
    f32 = jnp.float32
    bf16 = jnp.bfloat16
    rows = query.shape[0]
    heads_here = level_coef.shape[1]
    width = query.shape[1] // heads_here
    depth = level_coef.shape[0] - 1
    group = lax.axis_index("seq")
    q_three = query.reshape(rows, heads_here, width)
    k_three = key.reshape(rows, heads_here, width)
    v_three = value.reshape(rows, heads_here, width)
    scores = jnp.einsum("the,she->hts", q_three, k_three, preferred_element_type=f32)
    causal = lax.broadcasted_iota(jnp.int32, (rows, rows), 0) >= lax.broadcasted_iota(
        jnp.int32, (rows, rows), 1
    )
    kept = jnp.where(causal[None], scores, 0.0).astype(bf16)
    local = jnp.einsum("hts,she->the", kept, v_three, preferred_element_type=f32)
    states = jnp.einsum("sha,shb->hab", k_three, v_three, preferred_element_type=f32)
    bits = [(group // 2**level % 2).astype(f32) for level in range(depth)]
    block = states
    found = []
    for level in range(depth):
        other = from_partner(block, "seq", level)
        found.append(bits[level] * other)
        block = block + other
    buckets = jnp.stack(found)
    bucket_half = buckets.astype(bf16)
    reads = jnp.einsum("the,lhef->lthf", q_three, bucket_half, preferred_element_type=f32)
    first = level_coef[0].T[:, :, None]
    rest = level_coef[1:].transpose(0, 2, 1)[..., None]
    output = first * local + jnp.sum(rest * reads, axis=0)
    squares = lax.psum(jnp.sum(output * output, axis=(1, 2)), "head")
    scale = lax.rsqrt(squares / (HEADS * HEAD_DIM) + EPS)[:, None, None]
    normed = output * scale
    gain_three = gain.reshape(heads_here, width)
    mixed = (normed * gain_three).astype(bf16).reshape(rows, -1)
    cot_three = cotangent.reshape(rows, heads_here, width).astype(f32)
    grad_gain = lax.psum(jnp.sum(cot_three * normed, axis=0).reshape(-1), "seq")
    weighted_cot = cot_three * gain_three
    inner = lax.psum(jnp.sum(weighted_cot * output, axis=(1, 2)), "head")
    grad_full = (
        weighted_cot - output * (inner[:, None, None] * scale * scale / (HEADS * HEAD_DIM))
    ) * scale
    grad_half = grad_full.astype(bf16)
    grad_float = grad_half.astype(f32)
    grad_first = jnp.sum(grad_float * local, axis=-1)
    grad_rest = jnp.sum(grad_float[None] * reads, axis=-1)
    grad_level = jnp.concatenate([grad_first.T[None], grad_rest.transpose(0, 2, 1)], axis=0)
    weighted = (first * grad_float).astype(bf16)
    value_sum = jnp.einsum("hts,the->she", kept, weighted, preferred_element_type=f32)
    pair = (
        jnp.einsum("the,she->hts", grad_half, v_three, preferred_element_type=f32)
        * level_coef[0][:, :, None]
    )
    pair = jnp.where(causal[None], pair, 0.0).astype(bf16)
    query_sum = jnp.einsum("hts,she->the", pair, k_three, preferred_element_type=f32)
    key_sum = jnp.einsum("hts,the->she", pair, q_three, preferred_element_type=f32)
    scaled = (rest * grad_float[None]).astype(bf16)
    query_sum = query_sum + jnp.einsum(
        "lthf,lhef->the", scaled, bucket_half, preferred_element_type=f32
    )
    grad_buckets = jnp.einsum("the,lthf->lhef", q_three, scaled, preferred_element_type=f32)
    masks = jnp.stack(bits)[:, None, None, None]
    pending = masks * grad_buckets
    carried = jnp.zeros_like(states)
    for level in range(depth):
        other = from_partner(pending, "seq", level)
        carried = carried + (1.0 - bits[level]) * other[0]
        pending = pending[1:] + other[1:]
    grad_states = carried.astype(bf16)
    key_sum = key_sum + jnp.einsum("shb,hab->sha", v_three, grad_states, preferred_element_type=f32)
    value_sum = value_sum + jnp.einsum(
        "sha,hab->shb", k_three, grad_states, preferred_element_type=f32
    )
    grad_query = query_sum.astype(bf16).reshape(rows, -1)
    grad_key = key_sum.astype(bf16).reshape(rows, -1)
    grad_value = value_sum.astype(bf16).reshape(rows, -1)
    return (mixed, grad_query, grad_key, grad_value, grad_level, grad_gain)


def solution(mesh):
    placed = (
        P("seq", "head"),
        P("seq", "head"),
        P("seq", "head"),
        P(None, "head", "seq"),
        P("head"),
        P("seq", "head"),
    )
    return jax.shard_map(
        body,
        mesh=mesh,
        in_specs=placed,
        out_specs=(
            P("seq", "head"),
            P("seq", "head"),
            P("seq", "head"),
            P("seq", "head"),
            P(None, "head", "seq"),
            P("head"),
        ),
        check_vma=False,
    )
```

profile of v0, /device:TPU:0, one launch (start us, length us, event | category | flops | bytes accessed | tf_op | source)
XLA Modules:
  0.0 245.2 jit_solution(4690820925191589461)
XLA Ops:
  0.6 0.0 copy-start
  0.6 3.7 %copy.75 = bf16[128,8,8,128]{3,2,1,0:T(8,128)(2,1)} copy(bf16[128,8,8,128]{3,1,2,0:T(8,128)(2,1)} %bitcast.130) | data formatting | bytes 4194304
  4.3 4.1 %copy.39 = bf16[1024,8,128]{0,2,1:T(8,128)(2,1)} copy(bf16[1024,8,128]{2,1,0:T(8,128)(2,1)} %bitcast.129) | data formatting | bytes 4194304 | tf_op jit(solution)/shard_map/reshape | solution.py:30
  8.4 0.0 copy-done
  8.4 2.3 fusion.15
  10.8 0.0 copy-start.5
  10.8 3.1 %collective-permute-start = (f32[8,128,128]{2,1,0:T(8,128)S(1)}, f32[8,128,128]{2,1,0:T(8,128)}, u32[]{:S(2)}, u32[]{:S(2)}) collective-permute-start(f32[8,128,128]{2,1,0:T(8,128)S(1)} %fusion.15), channel_id=1, source_target_pairs={{0,4},{4,0},{8,12},{12,8},{16,20},{20,16},{24,28},{28,24},{1,5},{5... | collective-permute-start | bytes 1572872 | tf_op jit(solution)/shard_map/ppermute | solution.py:18
  13.9 3.5 %copy.74 = bf16[128,8,8,128]{3,2,1,0:T(8,128)(2,1)} copy(bf16[128,8,8,128]{3,1,2,0:T(8,128)(2,1)} %bitcast.133) | data formatting | bytes 4194304
  17.4 4.1 %copy.49 = bf16[1024,8,128]{0,2,1:T(8,128)(2,1)} copy(bf16[1024,8,128]{2,1,0:T(8,128)(2,1)} %bitcast.122) | data formatting | bytes 4194304 | tf_op jit(solution)/shard_map/reshape | solution.py:29
  21.5 0.0 copy-done.5
  21.5 0.3 iota_compare_fusion
  21.8 0.0 copy-start.3
  21.8 4.1 %collective-permute-done = f32[8,128,128]{2,1,0:T(8,128)} collective-permute-done((f32[8,128,128]{2,1,0:T(8,128)S(1)}, f32[8,128,128]{2,1,0:T(8,128)}, u32[]{:S(2)}, u32[]{:S(2)}) %collective-permute-start) | collective-permute-done | bytes 524320 | tf_op jit(solution)/shard_map/ppermute | solution.py:18
  25.9 1.3 fusion.37
  27.2 0.0 copy-start.6
  27.2 1.9 collective-permute-start.1
  29.1 0.0 copy-done.3
  29.1 10.4 %select_convert_fusion.1 = bf16[8,1024,1024]{2,1,0:T(8,128)(2,1)} fusion(pred[1024,1024]{1,0:T(8,128)(4,1)S(1)} %iota_compare_fusion, bf16[1024,8,128]{0,2,1:T(8,128)(2,1)} %copy.49, bf16[1024,1024]{1,0:T(8,128)(2,1)} %param.7), kind=kOutput, calls=%fused_computation.1 | convolution fusion | flops 2164260864 | bytes 22020096 | tf_op jit(solution)/shard_map/the,she->hts/dot_general | solution.py:32
  39.4 1.0 collective-permute-done.1
  40.4 1.9 fusion.38
  42.4 2.5 %collective-permute-start.2 = (f32[8,128,128]{2,1,0:T(8,128)}, f32[8,128,128]{2,1,0:T(8,128)}, u32[]{:S(2)}, u32[]{:S(2)}) collective-permute-start(f32[8,128,128]{2,1,0:T(8,128)} %get-tuple-element.30), channel_id=1, source_target_pairs={{0,16},{16,0},{4,20},{20,4},{8,24},{24,8},{12,28},{28,12},{1,17},{... | collective-permute-start | bytes 1572872 | tf_op jit(solution)/shard_map/ppermute | solution.py:18
  44.9 0.0 copy-done.6
  44.9 0.1 copy.38
  45.0 4.1 %copy.43 = f32[1024,1024]{0,1:T(8,128)} copy(bf16[1024,1024]{1,0:T(8,128)(2,1)} %param.11) | data formatting | bytes 6291456 | tf_op jit(solution)/shard_map/convert_element_type | solution.py:57
  49.1 0.1 pad_maximum_fusion.2
  49.2 17.9 %collective-permute-done.2 = f32[8,128,128]{2,1,0:T(8,128)} collective-permute-done((f32[8,128,128]{2,1,0:T(8,128)}, f32[8,128,128]{2,1,0:T(8,128)}, u32[]{:S(2)}, u32[]{:S(2)}) %collective-permute-start.2) | collective-permute-done | bytes 524320 | tf_op jit(solution)/shard_map/ppermute | solution.py:18
  67.0 1.1 fusion.39
  68.1 10.4 %fusion = (f32[1024,8,128]{0,2,1:T(8,128)}, f32[8,3,128,1024]{3,2,1,0:T(8,128)}) fusion(f32[3,1024,8]{1,0,2:T(4,128)S(1)} %copy.38, bf16[1024,8,128,1]{2,1,0,3:T(8,128)(2,1)} %bitcast.123, bf16[1,8,128,128]{3,2,1,0:T(8,128)(2,1)S(1)} %fusion.39, bf16[1,8,128,128]{3,2,1,0:T(8,128)(2,1)S(1)} %get-tuple-element.29, ...), kind=kOutput, calls=%fused_computation.4 | convolution fusion | flops 811335680 | bytes 19759104 | tf_op jit(solution)/shard_map/the,lhef->lthf/dot_general | solution.py:48
  78.5 12.1 %multiply_reduce_fusion.2 = (f32[1024]{0:T(1024)S(1)}, f32[1024,8,128]{0,2,1:T(8,128)}, f32[8,1024,128]{1,2,0:T(8,128)}) fusion(f32[1024,8,128]{0,2,1:T(8,128)} %get-tuple-element.33, f32[1024,8]{0,1:T(8,128)S(1)} %get-tuple-element.32, bf16[8,1024,1024]{2,1,0:T(8,128)(2,1)} %select_convert_fusion.1, bf16[1024,1024]{1,0:T(8,128)(2,1)S(1)} %copy-done), kind=kOutput, calls=%fused_computation.23 | convolution fusion | flops 2151676928 | bytes 31494144 | tf_op jit(solution)/shard_map/hts,she->the/dot_general | solution.py:37
  90.6 5.6 %psum.21 = f32[1024]{0:T(1024)S(1)} all-reduce(f32[1024]{0:T(1024)S(1)} %get-tuple-element.22), channel_id=1, replica_groups=mesh['seq'=8,'head'=4] {'head'}, use_global_device_ids=true, to_apply=%region_2.3 | all-reduce | flops 1024 | bytes 8192 | tf_op jit(solution)/shard_map/psum | solution.py:52
  96.2 0.0 copy-done.7
  96.2 5.7 %multiply_reduce_fusion = (f32[8,128]{1,0:T(8,128)S(1)}, f32[1024]{0:T(1024)S(1)}) fusion(f32[1024,8,128]{0,2,1:T(8,128)} %bitcast.121, f32[1024,8,128]{0,2,1:T(8,128)} %get-tuple-element.23, f32[1024]{0:T(1024)S(1)} %add_rsqrt_fusion, f32[8,128]{1,0:T(8,128)S(1)} %bitcast.136, f32[1024,1024]{0,1:T(8,128)} %copy.43), kind=kLoop, calls=%fused_computation.17 | loop fusion | flops 6289408 | bytes 12599296 | tf_op jit(solution)/shard_map/reduce_sum | solution.py:58
  101.9 6.5 %psum.22 = f32[1024]{0:T(1024)S(1)} all-reduce(f32[1024]{0:T(1024)S(1)} %get-tuple-element.19), channel_id=1, replica_groups=mesh['seq'=8,'head'=4] {'head'}, use_global_device_ids=true, to_apply=%region_4.5 | all-reduce | flops 1024 | bytes 8192 | tf_op jit(solution)/shard_map/psum | solution.py:60
  108.5 0.0 slice-start.2
  108.5 6.7 %fusion.7 = (f32[1024,8]{0,1:T(8,128)S(1)}, bf16[1024,8,128]{0,2,1:T(8,128)(2,1)S(1)}, bf16[1024,8,128]{0,2,1:T(8,128)(2,1)}) fusion(f32[8,1024,128]{1,2,0:T(8,128)} %get-tuple-element.35, f32[1024]{0:T(1024)S(1)} %add_rsqrt_fusion, f32[1024,8,128]{0,2,1:T(8,128)} %get-tuple-element.23, f32[1024]{0:T(1024)S(1)} %fusion.41, f32[8,128]{1,0:T(8,128)S(1)} %bitcast.137, ...), kind=kLoop, calls=%fused_computation.16 | loop fusion | flops 11526144 | bytes 16822272 | tf_op jit(solution)/shard_map/reduce_sum | solution.py:66
  115.2 0.4 convert_element_type.64
  115.7 1.0 slice-done.1
  116.7 1.6 slice-done.2
  118.3 4.3 %fusion.1 = (f32[3,1024,8]{1,0,2:T(4,128)S(1)}, bf16[3,1024,8,128]{1,3,0,2:T(8,128)(2,1)}) fusion(f32[8,3,128,1024]{3,2,1,0:T(8,128)S(1)} %bitcast.118, f32[1024,8,128]{0,2,1:T(8,128)S(1)} %convert_element_type.64, f32[3,1024,8]{1,0,2:T(4,128)S(1)} %copy.38), kind=kLoop, calls=%fused_computation.5 | loop fusion | flops 12558336 | bytes 23265280 | tf_op jit(solution)/shard_map/reduce_sum | solution.py:67
  122.6 0.1 pad_maximum_fusion.1
  122.7 0.7 copy.58
  123.4 3.0 %multiply_bitcast_fusion = f32[3,8,128,128]{2,3,0,1:T(8,128)} fusion(bf16[1024,8,128,1]{2,1,0,3:T(8,128)(2,1)S(1)} %bitcast.124, f32[3]{0:T(128)S(1)} %pad_maximum_fusion.2, f32[1024,8,128]{0,2,1:T(8,128)S(1)} %convert_element_type.64, f32[3,1024,8]{1,0,2:T(4,128)S(1)} %copy.38), kind=kOutput, calls=%fused_computation.42 | convolution fusion | flops 811991040 | bytes 7962636 | tf_op jit(solution)/shard_map/the,lthf->lhef/dot_general | solution.py:82
  126.4 1.3 collective-permute-start.3
  127.6 0.0 copy-done.2
  127.6 9.6 %select_convert_fusion = bf16[8,1024,1024]{2,1,0:T(8,128)(2,1)} fusion(f32[8,1024]{1,0:T(8,128)S(1)} %get-tuple-element.31, pred[1024,1024]{1,0:T(8,128)(4,1)S(1)} %copy-done.4, bf16[1024,8,128]{0,2,1:T(8,128)(2,1)S(1)} %get-tuple-element.21, bf16[1024,1024]{1,0:T(8,128)(2,1)S(1)} %copy-done), kind=kOutput, calls=%fused_computation | convolution fusion | flops 2172649472 | bytes 22052864 | tf_op jit(solution)/shard_map/the,she->hts/dot_general | solution.py:72
  137.3 11.4 %fusion.43 = f32[8,1024,128]{1,2,0:T(8,128)} fusion(bf16[8,1024,1024]{2,1,0:T(8,128)(2,1)} %select_convert_fusion, bf16[1024,8,128]{0,2,1:T(8,128)(2,1)} %copy.39), kind=kOutput, calls=%fused_computation.71 | convolution fusion | flops 2147483648 | bytes 23068672 | tf_op jit(solution)/shard_map/hts,she->the/dot_general | solution.py:76
  148.7 10.9 %fusion.10 = f32[8,128,1024]{2,1,0:T(8,128)} fusion(bf16[8,1024,1024]{2,1,0:T(8,128)(2,1)} %select_convert_fusion.1, bf16[1024,8,128]{0,2,1:T(8,128)(2,1)} %copy-done.2, f32[1024,8]{0,1:T(8,128)S(1)} %get-tuple-element.32), kind=kOutput, calls=%fused_computation.25 | convolution fusion | flops 2150629376 | bytes 23101440 | tf_op jit(solution)/shard_map/hts,the->she/dot_general | solution.py:70
  159.6 2.4 collective-permute-done.3
  162.0 2.8 %slice_add_fusion = f32[2,8,128,128]{2,3,0,1:T(8,128)} fusion(f32[3,8,128,128]{2,3,0,1:T(8,128)} %collective-permute-done.3, f32[3,8,128,128]{2,3,0,1:T(8,128)} %multiply_bitcast_fusion), kind=kLoop, calls=%fused_computation.47 | loop fusion | flops 262144 | bytes 3145728 | tf_op jit(solution)/shard_map/add | solution.py:89
  164.8 1.5 collective-permute-start.4
  166.3 6.1 %fusion.44 = f32[8,1024,128]{1,2,0:T(8,128)} fusion(bf16[1024,8,128]{0,2,1:T(8,128)(2,1)} %copy.49, bf16[8,1024,1024]{2,1,0:T(8,128)(2,1)S(1)} %bitcast.120), kind=kOutput, calls=%fused_computation.72 | convolution fusion | flops 2147483648 | bytes 23068672 | tf_op jit(solution)/shard_map/hts,the->she/dot_general | solution.py:77
  172.4 16.3 %collective-permute-done.4 = f32[2,8,128,128]{2,3,0,1:T(8,128)} collective-permute-done((f32[2,8,128,128]{2,3,0,1:T(8,128)}, f32[2,8,128,128]{2,3,0,1:T(8,128)}, u32[]{:S(2)}, u32[]{:S(2)}) %collective-permute-start.4) | collective-permute-done | bytes 1048608 | tf_op jit(solution)/shard_map/ppermute | solution.py:18
  188.7 1.3 slice_add_fusion.1
  190.0 3.4 %collective-permute-start.5 = (f32[1,8,128,128]{2,3,0,1:T(8,128)S(1)}, f32[1,8,128,128]{2,3,0,1:T(8,128)}, u32[]{:S(2)}, u32[]{:S(2)}) collective-permute-start(f32[1,8,128,128]{2,3,0,1:T(8,128)S(1)} %slice_add_fusion.1), channel_id=1, source_target_pairs={{0,16},{16,0},{4,20},{20,4},{8,24},{24,8},{12,28},{28,12},{1,17},{... | collective-permute-start | bytes 1572872 | tf_op jit(solution)/shard_map/ppermute | solution.py:18
  193.4 4.8 %fusion.4 = bf16[1024,8,128]{0,2,1:T(8,128)(2,1)} fusion(f32[8,1024,128]{1,2,0:T(8,128)} %fusion.43, bf16[3,1024,8,128]{1,3,0,2:T(8,128)(2,1)S(1)} %bitcast.126, bf16[1,8,128,128]{3,2,1,0:T(8,128)(2,1)S(1)} %fusion.39, bf16[1,8,128,128]{3,2,1,0:T(8,128)(2,1)S(1)} %get-tuple-element.29, bf16[1,8,128,128]{3,2,1,0:T(8,128)(2,1)S(1)} %get-tuple-element.27), kind=kOutput, calls=%fused_computation.10 | convolution fusion | flops 808189952 | bytes 13369344 | tf_op jit(solution)/shard_map/lthf,lhef->the/dot_general | solution.py:79
  198.2 3.9 %copy.55 = bf16[1024,1024]{1,0:T(8,128)(2,1)} copy(bf16[1024,1024]{0,1:T(8,128)(2,1)} %bitcast.128) | data formatting | bytes 4194304
  202.1 3.9 %copy.54 = bf16[1024,1024]{1,0:T(8,128)(2,1)} copy(bf16[1024,1024]{0,1:T(8,128)(2,1)} %bitcast.127) | data formatting | bytes 4194304
  206.0 20.6 %psum.23 = f32[1024]{0:T(1024)} all-reduce(f32[1024]{0:T(1024)S(1)} %bitcast.138), channel_id=1, replica_groups=mesh['seq'=8,'head'=4] {'seq'}, use_global_device_ids=true, to_apply=%region_8.9 | all-reduce | flops 1024 | bytes 8192 | tf_op jit(solution)/shard_map/psum | solution.py:58
  226.6 0.0 collective-permute-done.5
  226.6 1.5 fusion.40
  228.1 4.9 %add_convert_fusion = bf16[8,128,1024]{2,1,0:T(8,128)(2,1)} fusion(f32[8,128,1024]{2,1,0:T(8,128)} %fusion.10, bf16[8,128,128]{1,2,0:T(8,128)(2,1)S(1)} %fusion.40, bf16[1024,1024]{1,0:T(8,128)(2,1)} %param.7), kind=kOutput, calls=%fused_computation.18 | convolution fusion | flops 270532608 | bytes 8650752 | tf_op jit(solution)/shard_map/sha,hab->shb/dot_general | solution.py:92
  233.0 3.9 %copy.57 = bf16[1024,1024]{1,0:T(8,128)(2,1)} copy(bf16[1024,1024]{0,1:T(8,128)(2,1)} %bitcast.132) | data formatting | bytes 4194304
  236.9 4.3 %fusion.5 = bf16[1024,8,128]{0,2,1:T(8,128)(2,1)} fusion(f32[8,1024,128]{1,2,0:T(8,128)} %fusion.44, bf16[8,128,128]{1,2,0:T(8,128)(2,1)S(1)} %fusion.40, bf16[1024,1024]{1,0:T(8,128)(2,1)S(1)} %copy-done), kind=kOutput, calls=%fused_computation.12 | convolution fusion | flops 270532608 | bytes 8650752 | tf_op jit(solution)/shard_map/shb,hab->sha/dot_general | solution.py:91
  241.3 3.9 %copy.56 = bf16[1024,1024]{1,0:T(8,128)(2,1)} copy(bf16[1024,1024]{0,1:T(8,128)(2,1)} %bitcast.131) | data formatting | bytes 4194304
  (29 shorter events, 0.1 us)
Async XLA Ops:
  0.6 7.8 %copy-start = (bf16[1024,1024]{1,0:T(8,128)(2,1)S(1)}, bf16[1024,1024]{1,0:T(8,128)(2,1)}, u32[]{:S(2)}) copy-start(bf16[1024,1024]{1,0:T(8,128)(2,1)} %param.8) | copy-start | bytes 6291460
  10.8 10.7 %copy-start.5 = (f32[8,128,128]{2,1,0:T(8,128)}, f32[8,128,128]{2,1,0:T(8,128)S(1)}, u32[]{:S(2)}) copy-start(f32[8,128,128]{2,1,0:T(8,128)S(1)} %fusion.15) | copy-start | bytes 1572868
  10.8 15.1 %collective-permute-start = (f32[8,128,128]{2,1,0:T(8,128)S(1)}, f32[8,128,128]{2,1,0:T(8,128)}, u32[]{:S(2)}, u32[]{:S(2)}) collective-permute-start(f32[8,128,128]{2,1,0:T(8,128)S(1)} %fusion.15), channel_id=1, source_target_pairs={{0,4},{4,0},{8,12},{12,8},{16,20},{20,16},{24,28},{28,24},{1,5},{5... | collective-permute-start | bytes 1572872 | tf_op jit(solution)/shard_map/ppermute | solution.py:18
  21.8 7.2 %copy-start.3 = (pred[1024,1024]{1,0:T(8,128)(4,1)}, pred[1024,1024]{1,0:T(8,128)(4,1)S(1)}, u32[]{:S(2)}) copy-start(pred[1024,1024]{1,0:T(8,128)(4,1)S(1)} %iota_compare_fusion) | copy-start | bytes 3145732
  27.2 17.7 %copy-start.6 = (f32[4,8,1024]{2,1,0:T(8,128)S(1)}, f32[4,8,1024]{2,1,0:T(8,128)}, u32[]{:S(2)}) copy-start(f32[4,8,1024]{2,1,0:T(8,128)} %param.9) | copy-start | bytes 393220
  27.2 13.3 %collective-permute-start.1 = (f32[8,128,128]{2,1,0:T(8,128)S(1)}, f32[8,128,128]{2,1,0:T(8,128)}, u32[]{:S(2)}, u32[]{:S(2)}) collective-permute-start(f32[8,128,128]{2,1,0:T(8,128)S(1)} %get-tuple-element.28), channel_id=1, source_target_pairs={{0,8},{8,0},{4,12},{12,4},{16,24},{24,16},{20,28},{28,20},{1,9},{9... | collective-permute-start | bytes 1572872 | tf_op jit(solution)/shard_map/ppermute | solution.py:18
  42.4 24.7 %collective-permute-start.2 = (f32[8,128,128]{2,1,0:T(8,128)}, f32[8,128,128]{2,1,0:T(8,128)}, u32[]{:S(2)}, u32[]{:S(2)}) collective-permute-start(f32[8,128,128]{2,1,0:T(8,128)} %get-tuple-element.30), channel_id=1, source_target_pairs={{0,16},{16,0},{4,20},{20,4},{8,24},{24,8},{12,28},{28,12},{1,17},{... | collective-permute-start | bytes 1572872 | tf_op jit(solution)/shard_map/ppermute | solution.py:18
  78.5 17.7 %copy-start.7 = (f32[1024]{0:T(1024)S(1)}, f32[1024]{0:T(1024)}, u32[]{:S(2)}) copy-start(f32[1024]{0:T(1024)} %param.10) | copy-start | bytes 12292
  108.5 7.2 %slice-start = ((s8[12582912]{0:T(1024)(128)(4,1)}), s8[4194304]{0:T(1024)(128)(4,1)S(1)}, s32[]{:S(2)}) async-start(s8[12582912]{0:T(1024)(128)(4,1)} %bitcast.117), calls=%async_computation | async-start | bytes 8388608
  108.5 8.2 %slice-start.1 = ((s8[12582912]{0:T(1024)(128)(4,1)}), s8[4194304]{0:T(1024)(128)(4,1)S(1)}, s32[]{:S(2)}) async-start(s8[12582912]{0:T(1024)(128)(4,1)} %bitcast.117), calls=%async_computation.1 | async-start | bytes 8388608
  108.5 9.8 %slice-start.2 = ((s8[12582912]{0:T(1024)(128)(4,1)}), s8[4194304]{0:T(1024)(128)(4,1)S(1)}, s32[]{:S(2)}) async-start(s8[12582912]{0:T(1024)(128)(4,1)} %bitcast.117), calls=%async_computation.2 | async-start | bytes 8388608
  115.2 12.4 %copy-start.2 = (bf16[1024,8,128]{0,2,1:T(8,128)(2,1)}, bf16[1024,8,128]{0,2,1:T(8,128)(2,1)S(1)}, u32[]{:S(2)}) copy-start(bf16[1024,8,128]{0,2,1:T(8,128)(2,1)S(1)} %get-tuple-element.21) | copy-start | bytes 6291460
  118.3 5.1 %copy-start.1 = (bf16[128,8,8,128]{3,2,1,0:T(8,128)(2,1)S(1)}, bf16[128,8,8,128]{3,2,1,0:T(8,128)(2,1)}, u32[]{:S(2)}) copy-start(bf16[128,8,8,128]{3,2,1,0:T(8,128)(2,1)} %copy.74) | copy-start | bytes 6291460
  123.4 4.2 %copy-start.4 = (pred[1024,1024]{1,0:T(8,128)(4,1)S(1)}, pred[1024,1024]{1,0:T(8,128)(4,1)}, u32[]{:S(2)}) copy-start(pred[1024,1024]{1,0:T(8,128)(4,1)} %copy-done.3) | copy-start | bytes 3145732
  126.4 35.6 %collective-permute-start.3 = (f32[3,8,128,128]{2,3,0,1:T(8,128)}, f32[3,8,128,128]{2,3,0,1:T(8,128)}, u32[]{:S(2)}, u32[]{:S(2)}) collective-permute-start(f32[3,8,128,128]{2,3,0,1:T(8,128)} %multiply_bitcast_fusion), channel_id=1, source_target_pairs={{0,4},{4,0},{8,12},{12,8},{16,20},{20,16},{24,28},{28,24},{1,5},{5... | collective-permute-start | bytes 4718600 | tf_op jit(solution)/shard_map/ppermute | solution.py:18
  137.3 29.0 %slice-start.3 = ((s8[16777216]{0:T(1024)(128)(4,1)}), s8[4194304]{0:T(1024)(128)(4,1)S(1)}, s32[]{:S(2)}) async-start(s8[16777216]{0:T(1024)(128)(4,1)} %bitcast.119), calls=%async_computation.3 | async-start | bytes 8388608
  137.3 29.0 %slice-start.4 = ((s8[16777216]{0:T(1024)(128)(4,1)}), s8[4194304]{0:T(1024)(128)(4,1)S(1)}, s32[]{:S(2)}) async-start(s8[16777216]{0:T(1024)(128)(4,1)} %bitcast.119), calls=%async_computation.4 | async-start | bytes 8388608
  137.3 29.0 %slice-start.5 = ((s8[16777216]{0:T(1024)(128)(4,1)}), s8[4194304]{0:T(1024)(128)(4,1)S(1)}, s32[]{:S(2)}) async-start(s8[16777216]{0:T(1024)(128)(4,1)} %bitcast.119), calls=%async_computation.5 | async-start | bytes 8388608
  148.7 17.6 %slice-start.6 = ((s8[16777216]{0:T(1024)(128)(4,1)}), s8[4194304]{0:T(1024)(128)(4,1)S(1)}, s32[]{:S(2)}) async-start(s8[16777216]{0:T(1024)(128)(4,1)} %bitcast.119), calls=%async_computation.6 | async-start | bytes 8388608
  162.0 31.4 %slice-start.7 = ((s8[6291456]{0:T(1024)(128)(4,1)}), s8[4194304]{0:T(1024)(128)(4,1)S(1)}, s32[]{:S(2)}) async-start(s8[6291456]{0:T(1024)(128)(4,1)} %bitcast.125), calls=%async_computation.7 | async-start | bytes 8388608
  164.8 28.6 %slice-start.8 = ((s8[6291456]{0:T(1024)(128)(4,1)}), s8[2097152]{0:T(1024)(128)(4,1)S(1)}, s32[]{:S(2)}) async-start(s8[6291456]{0:T(1024)(128)(4,1)} %bitcast.125), calls=%async_computation.8 | async-start | bytes 4194304
  164.8 23.9 %collective-permute-start.4 = (f32[2,8,128,128]{2,3,0,1:T(8,128)}, f32[2,8,128,128]{2,3,0,1:T(8,128)}, u32[]{:S(2)}, u32[]{:S(2)}) collective-permute-start(f32[2,8,128,128]{2,3,0,1:T(8,128)} %slice_add_fusion), channel_id=1, source_target_pairs={{0,8},{8,0},{4,12},{12,4},{16,24},{24,16},{20,28},{28,20},{1,9},{9... | collective-permute-start | bytes 3145736 | tf_op jit(solution)/shard_map/ppermute | solution.py:18
  190.0 36.7 %collective-permute-start.5 = (f32[1,8,128,128]{2,3,0,1:T(8,128)S(1)}, f32[1,8,128,128]{2,3,0,1:T(8,128)}, u32[]{:S(2)}, u32[]{:S(2)}) collective-permute-start(f32[1,8,128,128]{2,3,0,1:T(8,128)S(1)} %slice_add_fusion.1), channel_id=1, source_target_pairs={{0,16},{16,0},{4,20},{20,4},{8,24},{24,8},{12,28},{28,12},{1,17},{... | collective-permute-start | bytes 1572872 | tf_op jit(solution)/shard_map/ppermute | solution.py:18
where the time goes:
time: 246 us; the launch traced here: 245 us
  matrix products  90.1 us (37%)
  waiting for transfers between devices  41.6 us (17%)
  local copies, waits for them, and re-layouts  38.8 us (16%)
  blocking collectives  32.7 us (13%)
  other arithmetic  27.4 us (11%)
  starting transfers between devices  13.7 us (6%)
    ppermute x6, waiting for transfers between devices, from_partner(): return lax.ppermute(block, axis, route)  41.6 us
    unnamed x41, local copies, waits for them, and re-layouts  26.4 us
    psum x1, blocking collectives, body(): grad_gain = lax.psum(jnp.sum(cot_three * normed, axis=0).reshape(-1), 'seq')  20.6 us
    ppermute x6, starting transfers between devices, from_partner(): return lax.ppermute(block, axis, route)  13.7 us
    dot_general x1, matrix products, body(): jnp.einsum('hts,she->the', kept, v_three, preferred_element_type=f32)  12.1 us
    dot_general x1, matrix products, body(): jnp.einsum('hts,she->the', pair, k_three, preferred_element_type=f32)  11.4 us
    dot_general x1, matrix products, body(): jnp.einsum('hts,the->she', kept, weighted, preferred_element_type=f32)  10.9 us
    dot_general x1, matrix products, body(): jnp.einsum('the,she->hts', q_three, k_three, preferred_element_type=f32)  10.4 us
  transfers between devices with their start and end apart: 6, of which 5 were waited for; matrix products, arithmetic and copies ran while one was open for 30% of the time, Pallas kernels for 0%

commit v1 on v0

--- a/solution.py
+++ b/solution.py
@@ -55,7 +55,9 @@
     gain_three = gain.reshape(heads_here, width)
     mixed = (normed * gain_three).astype(bf16).reshape(rows, -1)
     cot_three = cotangent.reshape(rows, heads_here, width).astype(f32)
-    grad_gain = lax.psum(jnp.sum(cot_three * normed, axis=0).reshape(-1), "seq")
+    grad_gain = jnp.sum(
+        lax.all_gather(jnp.sum(cot_three * normed, axis=0).reshape(-1), "seq"), axis=0
+    )
     weighted_cot = cot_three * gain_three
     inner = lax.psum(jnp.sum(weighted_cot * output, axis=(1, 2)), "head")
     grad_full = (

time: 246 us -> 257 us (1.045)
  blocking collectives: 32.7 us -> 43.3 us
    all_gather x0 -> x1, blocking collectives: none -> 31.2 us  [body(): lax.all_gather(jnp.sum(cot_three * normed, axis=0).reshape(-1), 'seq')]
    psum x1 -> x0, blocking collectives: 20.6 us -> none  [body(): grad_gain = lax.psum(jnp.sum(cot_three * normed, axis=0).reshape(-1), 'seq')]
    reduce_sum x1 -> x2, other arithmetic: 5.73 us -> 6.35 us  [the longest x1 5.73 us: body(): jnp.sum(cot_three * normed, axis=0).reshape(-1)]
  transfers between devices with their start and end apart: 6 -> 6, of which waited for: 5 -> 5; matrix products, arithmetic and copies ran while one was open for 30% -> 29% of each run, Pallas kernels for 0% -> 0%
where the time goes in v1:
time: 257 us; the launch traced here: 256 us
  matrix products  90.1 us (35%)
  blocking collectives  43.3 us (17%)
  waiting for transfers between devices  41.6 us (16%)
  local copies, waits for them, and re-layouts  38.8 us (15%)
  other arithmetic  28 us (11%)
  starting transfers between devices  13.7 us (5%)
    ppermute x6, waiting for transfers between devices, from_partner(): return lax.ppermute(block, axis, route)  41.6 us
    all_gather x1, blocking collectives, body(): lax.all_gather(jnp.sum(cot_three * normed, axis=0).reshape(-1), 'seq')  31.2 us
    unnamed x41, local copies, waits for them, and re-layouts  26.4 us
    ppermute x6, starting transfers between devices, from_partner(): return lax.ppermute(block, axis, route)  13.7 us
    dot_general x1, matrix products, body(): jnp.einsum('hts,she->the', kept, v_three, preferred_element_type=f32)  12.1 us
    dot_general x1, matrix products, body(): jnp.einsum('hts,she->the', pair, k_three, preferred_element_type=f32)  11.4 us
    dot_general x1, matrix products, body(): jnp.einsum('hts,the->she', kept, weighted, preferred_element_type=f32)  10.9 us
    dot_general x1, matrix products, body(): jnp.einsum('the,she->hts', q_three, k_three, preferred_element_type=f32)  10.4 us
  transfers between devices with their start and end apart: 6, of which 5 were waited for; matrix products, arithmetic and copies ran while one was open for 29% of the time, Pallas kernels for 0%

profile of v1, /device:TPU:0, one launch (start us, length us, event | category | flops | bytes accessed | tf_op | source)
XLA Modules:
  0.0 256.5 jit_solution(8038491470330482446)
XLA Ops:
  0.6 0.0 copy-start
  0.6 3.7 %copy.75 = bf16[128,8,8,128]{3,2,1,0:T(8,128)(2,1)} copy(bf16[128,8,8,128]{3,1,2,0:T(8,128)(2,1)} %bitcast.130) | data formatting | bytes 4194304
  4.3 4.1 %copy.39 = bf16[1024,8,128]{0,2,1:T(8,128)(2,1)} copy(bf16[1024,8,128]{2,1,0:T(8,128)(2,1)} %bitcast.129) | data formatting | bytes 4194304 | tf_op jit(solution)/shard_map/reshape | solution.py:30
  8.4 0.0 copy-done
  8.4 2.3 fusion.15
  10.8 0.0 copy-start.5
  10.8 3.1 %collective-permute-start = (f32[8,128,128]{2,1,0:T(8,128)S(1)}, f32[8,128,128]{2,1,0:T(8,128)}, u32[]{:S(2)}, u32[]{:S(2)}) collective-permute-start(f32[8,128,128]{2,1,0:T(8,128)S(1)} %fusion.15), channel_id=1, source_target_pairs={{0,4},{4,0},{8,12},{12,8},{16,20},{20,16},{24,28},{28,24},{1,5},{5... | collective-permute-start | bytes 1572872 | tf_op jit(solution)/shard_map/ppermute | solution.py:18
  13.9 3.5 %copy.74 = bf16[128,8,8,128]{3,2,1,0:T(8,128)(2,1)} copy(bf16[128,8,8,128]{3,1,2,0:T(8,128)(2,1)} %bitcast.133) | data formatting | bytes 4194304
  17.4 4.1 %copy.49 = bf16[1024,8,128]{0,2,1:T(8,128)(2,1)} copy(bf16[1024,8,128]{2,1,0:T(8,128)(2,1)} %bitcast.122) | data formatting | bytes 4194304 | tf_op jit(solution)/shard_map/reshape | solution.py:29
  21.5 0.0 copy-done.5
  21.5 0.3 iota_compare_fusion
  21.8 0.0 copy-start.3
  21.8 4.1 %collective-permute-done = f32[8,128,128]{2,1,0:T(8,128)} collective-permute-done((f32[8,128,128]{2,1,0:T(8,128)S(1)}, f32[8,128,128]{2,1,0:T(8,128)}, u32[]{:S(2)}, u32[]{:S(2)}) %collective-permute-start) | collective-permute-done | bytes 524320 | tf_op jit(solution)/shard_map/ppermute | solution.py:18
  25.9 1.3 fusion.37
  27.2 0.0 copy-start.6
  27.2 1.9 collective-permute-start.1
  29.1 0.0 copy-done.3
  29.1 10.4 %select_convert_fusion.1 = bf16[8,1024,1024]{2,1,0:T(8,128)(2,1)} fusion(pred[1024,1024]{1,0:T(8,128)(4,1)S(1)} %iota_compare_fusion, bf16[1024,8,128]{0,2,1:T(8,128)(2,1)} %copy.49, bf16[1024,1024]{1,0:T(8,128)(2,1)} %param.7), kind=kOutput, calls=%fused_computation.1 | convolution fusion | flops 2164260864 | bytes 22020096 | tf_op jit(solution)/shard_map/the,she->hts/dot_general | solution.py:32
  39.4 1.0 collective-permute-done.1
  40.4 1.9 fusion.38
  42.4 2.5 collective-permute-start.2
  44.9 0.0 copy-done.6
  44.9 0.1 copy.38
  45.0 4.1 %copy.43 = f32[1024,1024]{0,1:T(8,128)} copy(bf16[1024,1024]{1,0:T(8,128)(2,1)} %param.11) | data formatting | bytes 6291456 | tf_op jit(solution)/shard_map/convert_element_type | solution.py:57
  49.1 0.1 pad_maximum_fusion.2
  49.2 17.9 %collective-permute-done.2 = f32[8,128,128]{2,1,0:T(8,128)} collective-permute-done((f32[8,128,128]{2,1,0:T(8,128)}, f32[8,128,128]{2,1,0:T(8,128)}, u32[]{:S(2)}, u32[]{:S(2)}) %collective-permute-start.2) | collective-permute-done | bytes 524320 | tf_op jit(solution)/shard_map/ppermute | solution.py:18
  67.0 1.1 fusion.39
  68.1 10.4 %fusion = (f32[1024,8,128]{0,2,1:T(8,128)}, f32[8,3,128,1024]{3,2,1,0:T(8,128)}) fusion(f32[3,1024,8]{1,0,2:T(4,128)S(1)} %copy.38, bf16[1024,8,128,1]{2,1,0,3:T(8,128)(2,1)} %bitcast.123, bf16[1,8,128,128]{3,2,1,0:T(8,128)(2,1)S(1)} %fusion.39, bf16[1,8,128,128]{3,2,1,0:T(8,128)(2,1)S(1)} %get-tuple-element.29, ...), kind=kOutput, calls=%fused_computation.4 | convolution fusion | flops 811335680 | bytes 19759104 | tf_op jit(solution)/shard_map/the,lhef->lthf/dot_general | solution.py:48
  78.5 12.1 %multiply_reduce_fusion.2 = (f32[1024]{0:T(1024)S(1)}, f32[1024,8,128]{0,2,1:T(8,128)}, f32[8,1024,128]{1,2,0:T(8,128)}) fusion(f32[1024,8,128]{0,2,1:T(8,128)} %get-tuple-element.33, f32[1024,8]{0,1:T(8,128)S(1)} %get-tuple-element.32, bf16[8,1024,1024]{2,1,0:T(8,128)(2,1)} %select_convert_fusion.1, bf16[1024,1024]{1,0:T(8,128)(2,1)S(1)} %copy-done), kind=kOutput, calls=%fused_computation.23 | convolution fusion | flops 2151676928 | bytes 31494144 | tf_op jit(solution)/shard_map/hts,she->the/dot_general | solution.py:37
  90.6 5.6 %psum.14 = f32[1024]{0:T(1024)S(1)} all-reduce(f32[1024]{0:T(1024)S(1)} %get-tuple-element.22), channel_id=1, replica_groups=mesh['seq'=8,'head'=4] {'head'}, use_global_device_ids=true, to_apply=%region_2.3 | all-reduce | flops 1024 | bytes 8192 | tf_op jit(solution)/shard_map/psum | solution.py:52
  96.2 5.7 %multiply_reduce_fusion = (f32[8,128]{1,0:T(8,128)S(1)}, f32[1024]{0:T(1024)S(1)}) fusion(f32[1024,8,128]{0,2,1:T(8,128)} %bitcast.121, f32[1024,8,128]{0,2,1:T(8,128)} %get-tuple-element.23, f32[1024]{0:T(1024)S(1)} %add_rsqrt_fusion, f32[8,128]{1,0:T(8,128)S(1)} %bitcast.136, f32[1024,1024]{0,1:T(8,128)} %copy.43), kind=kLoop, calls=%fused_computation.17 | loop fusion | flops 6289408 | bytes 12599296 | tf_op jit(solution)/shard_map/reduce_sum | solution.py:59
  101.9 6.5 %psum.15 = f32[1024]{0:T(1024)S(1)} all-reduce(f32[1024]{0:T(1024)S(1)} %get-tuple-element.19), channel_id=1, replica_groups=mesh['seq'=8,'head'=4] {'head'}, use_global_device_ids=true, to_apply=%region_4.5 | all-reduce | flops 1024 | bytes 8192 | tf_op jit(solution)/shard_map/psum | solution.py:62
  108.5 0.0 slice-start.2
  108.5 6.7 %fusion.7 = (f32[1024,8]{0,1:T(8,128)S(1)}, bf16[1024,8,128]{0,2,1:T(8,128)(2,1)S(1)}, bf16[1024,8,128]{0,2,1:T(8,128)(2,1)}) fusion(f32[8,1024,128]{1,2,0:T(8,128)} %get-tuple-element.35, f32[1024]{0:T(1024)S(1)} %add_rsqrt_fusion, f32[1024,8,128]{0,2,1:T(8,128)} %get-tuple-element.23, f32[1024]{0:T(1024)S(1)} %fusion.41, f32[8,128]{1,0:T(8,128)S(1)} %bitcast.137, ...), kind=kLoop, calls=%fused_computation.16 | loop fusion | flops 11526144 | bytes 16822272 | tf_op jit(solution)/shard_map/reduce_sum | solution.py:68
  115.2 0.4 convert_element_type.64
  115.7 1.0 slice-done.1
  116.7 1.6 slice-done.2
  118.3 4.3 %fusion.1 = (f32[3,1024,8]{1,0,2:T(4,128)S(1)}, bf16[3,1024,8,128]{1,3,0,2:T(8,128)(2,1)}) fusion(f32[8,3,128,1024]{3,2,1,0:T(8,128)S(1)} %bitcast.118, f32[1024,8,128]{0,2,1:T(8,128)S(1)} %convert_element_type.64, f32[3,1024,8]{1,0,2:T(4,128)S(1)} %copy.38), kind=kLoop, calls=%fused_computation.5 | loop fusion | flops 12558336 | bytes 23265280 | tf_op jit(solution)/shard_map/reduce_sum | solution.py:69
  122.6 0.1 pad_maximum_fusion.1
  122.7 0.7 copy.58
  123.4 3.0 %multiply_bitcast_fusion = f32[3,8,128,128]{2,3,0,1:T(8,128)} fusion(bf16[1024,8,128,1]{2,1,0,3:T(8,128)(2,1)S(1)} %bitcast.124, f32[3]{0:T(128)S(1)} %pad_maximum_fusion.2, f32[1024,8,128]{0,2,1:T(8,128)S(1)} %convert_element_type.64, f32[3,1024,8]{1,0,2:T(4,128)S(1)} %copy.38), kind=kOutput, calls=%fused_computation.42 | convolution fusion | flops 811991040 | bytes 7962636 | tf_op jit(solution)/shard_map/the,lthf->lhef/dot_general | solution.py:84
  126.4 1.3 collective-permute-start.3
  127.6 0.0 copy-done.2
  127.6 9.6 %select_convert_fusion = bf16[8,1024,1024]{2,1,0:T(8,128)(2,1)} fusion(f32[8,1024]{1,0:T(8,128)S(1)} %get-tuple-element.31, pred[1024,1024]{1,0:T(8,128)(4,1)S(1)} %copy-done.4, bf16[1024,8,128]{0,2,1:T(8,128)(2,1)S(1)} %get-tuple-element.21, bf16[1024,1024]{1,0:T(8,128)(2,1)S(1)} %copy-done), kind=kOutput, calls=%fused_computation | convolution fusion | flops 2172649472 | bytes 22052864 | tf_op jit(solution)/shard_map/the,she->hts/dot_general | solution.py:74
  137.3 11.4 %fusion.43 = f32[8,1024,128]{1,2,0:T(8,128)} fusion(bf16[8,1024,1024]{2,1,0:T(8,128)(2,1)} %select_convert_fusion, bf16[1024,8,128]{0,2,1:T(8,128)(2,1)} %copy.39), kind=kOutput, calls=%fused_computation.71 | convolution fusion | flops 2147483648 | bytes 23068672 | tf_op jit(solution)/shard_map/hts,she->the/dot_general | solution.py:78
  148.7 10.9 %fusion.10 = f32[8,128,1024]{2,1,0:T(8,128)} fusion(bf16[8,1024,1024]{2,1,0:T(8,128)(2,1)} %select_convert_fusion.1, bf16[1024,8,128]{0,2,1:T(8,128)(2,1)} %copy-done.2, f32[1024,8]{0,1:T(8,128)S(1)} %get-tuple-element.32), kind=kOutput, calls=%fused_computation.25 | convolution fusion | flops 2150629376 | bytes 23101440 | tf_op jit(solution)/shard_map/hts,the->she/dot_general | solution.py:72
  159.6 2.4 collective-permute-done.3
  162.0 2.8 %slice_add_fusion = f32[2,8,128,128]{2,3,0,1:T(8,128)} fusion(f32[3,8,128,128]{2,3,0,1:T(8,128)} %collective-permute-done.3, f32[3,8,128,128]{2,3,0,1:T(8,128)} %multiply_bitcast_fusion), kind=kLoop, calls=%fused_computation.47 | loop fusion | flops 262144 | bytes 3145728 | tf_op jit(solution)/shard_map/add | solution.py:91
  164.8 1.5 collective-permute-start.4
  166.3 6.1 %fusion.44 = f32[8,1024,128]{1,2,0:T(8,128)} fusion(bf16[1024,8,128]{0,2,1:T(8,128)(2,1)} %copy.49, bf16[8,1024,1024]{2,1,0:T(8,128)(2,1)S(1)} %bitcast.120), kind=kOutput, calls=%fused_computation.72 | convolution fusion | flops 2147483648 | bytes 23068672 | tf_op jit(solution)/shard_map/hts,the->she/dot_general | solution.py:79
  172.4 16.3 %collective-permute-done.4 = f32[2,8,128,128]{2,3,0,1:T(8,128)} collective-permute-done((f32[2,8,128,128]{2,3,0,1:T(8,128)}, f32[2,8,128,128]{2,3,0,1:T(8,128)}, u32[]{:S(2)}, u32[]{:S(2)}) %collective-permute-start.4) | collective-permute-done | bytes 1048608 | tf_op jit(solution)/shard_map/ppermute | solution.py:18
  188.7 1.3 slice_add_fusion.1
  190.0 3.4 %collective-permute-start.5 = (f32[1,8,128,128]{2,3,0,1:T(8,128)S(1)}, f32[1,8,128,128]{2,3,0,1:T(8,128)}, u32[]{:S(2)}, u32[]{:S(2)}) collective-permute-start(f32[1,8,128,128]{2,3,0,1:T(8,128)S(1)} %slice_add_fusion.1), channel_id=1, source_target_pairs={{0,16},{16,0},{4,20},{20,4},{8,24},{24,8},{12,28},{28,12},{1,17},{... | collective-permute-start | bytes 1572872 | tf_op jit(solution)/shard_map/ppermute | solution.py:18
  193.4 4.8 %fusion.4 = bf16[1024,8,128]{0,2,1:T(8,128)(2,1)} fusion(f32[8,1024,128]{1,2,0:T(8,128)} %fusion.43, bf16[3,1024,8,128]{1,3,0,2:T(8,128)(2,1)S(1)} %bitcast.126, bf16[1,8,128,128]{3,2,1,0:T(8,128)(2,1)S(1)} %fusion.39, bf16[1,8,128,128]{3,2,1,0:T(8,128)(2,1)S(1)} %get-tuple-element.29, bf16[1,8,128,128]{3,2,1,0:T(8,128)(2,1)S(1)} %get-tuple-element.27), kind=kOutput, calls=%fused_computation.10 | convolution fusion | flops 808189952 | bytes 13369344 | tf_op jit(solution)/shard_map/lthf,lhef->the/dot_general | solution.py:81
  198.2 3.9 %copy.55 = bf16[1024,1024]{1,0:T(8,128)(2,1)} copy(bf16[1024,1024]{0,1:T(8,128)(2,1)} %bitcast.128) | data formatting | bytes 4194304
  202.1 3.9 %copy.54 = bf16[1024,1024]{1,0:T(8,128)(2,1)} copy(bf16[1024,1024]{0,1:T(8,128)(2,1)} %bitcast.127) | data formatting | bytes 4194304
  206.0 31.2 %all-gather = f32[8,1,1024]{2,1,0:T(1,128)S(1)} all-gather(f32[1,1,1024]{2,1,0:T(1,128)S(1)} %bitcast.138), channel_id=1, replica_groups=mesh['seq'=8,'head'=4] {'seq'}, dimensions={0}, use_global_device_ids=true | all-gather | bytes 36864 | tf_op jit(solution)/shard_map/all_gather | solution.py:59
  237.2 0.6 reduce_sum.69
  237.8 0.0 collective-permute-done.5
  237.8 1.5 fusion.40
  239.3 4.9 %add_convert_fusion = bf16[8,128,1024]{2,1,0:T(8,128)(2,1)} fusion(f32[8,128,1024]{2,1,0:T(8,128)} %fusion.10, bf16[8,128,128]{1,2,0:T(8,128)(2,1)S(1)} %fusion.40, bf16[1024,1024]{1,0:T(8,128)(2,1)} %param.7), kind=kOutput, calls=%fused_computation.18 | convolution fusion | flops 270532608 | bytes 8650752 | tf_op jit(solution)/shard_map/sha,hab->shb/dot_general | solution.py:94
  244.2 3.9 %copy.57 = bf16[1024,1024]{1,0:T(8,128)(2,1)} copy(bf16[1024,1024]{0,1:T(8,128)(2,1)} %bitcast.132) | data formatting | bytes 4194304
  248.2 4.3 %fusion.5 = bf16[1024,8,128]{0,2,1:T(8,128)(2,1)} fusion(f32[8,1024,128]{1,2,0:T(8,128)} %fusion.44, bf16[8,128,128]{1,2,0:T(8,128)(2,1)S(1)} %fusion.40, bf16[1024,1024]{1,0:T(8,128)(2,1)S(1)} %copy-done), kind=kOutput, calls=%fused_computation.12 | convolution fusion | flops 270532608 | bytes 8650752 | tf_op jit(solution)/shard_map/shb,hab->sha/dot_general | solution.py:93
  252.5 3.9 %copy.56 = bf16[1024,1024]{1,0:T(8,128)(2,1)} copy(bf16[1024,1024]{0,1:T(8,128)(2,1)} %bitcast.131) | data formatting | bytes 4194304
  (30 shorter events, 0.1 us)
Async XLA Ops:
  0.6 7.8 %copy-start = (bf16[1024,1024]{1,0:T(8,128)(2,1)S(1)}, bf16[1024,1024]{1,0:T(8,128)(2,1)}, u32[]{:S(2)}) copy-start(bf16[1024,1024]{1,0:T(8,128)(2,1)} %param.8) | copy-start | bytes 6291460
  10.8 10.7 %copy-start.5 = (f32[8,128,128]{2,1,0:T(8,128)}, f32[8,128,128]{2,1,0:T(8,128)S(1)}, u32[]{:S(2)}) copy-start(f32[8,128,128]{2,1,0:T(8,128)S(1)} %fusion.15) | copy-start | bytes 1572868
  10.8 15.1 %collective-permute-start = (f32[8,128,128]{2,1,0:T(8,128)S(1)}, f32[8,128,128]{2,1,0:T(8,128)}, u32[]{:S(2)}, u32[]{:S(2)}) collective-permute-start(f32[8,128,128]{2,1,0:T(8,128)S(1)} %fusion.15), channel_id=1, source_target_pairs={{0,4},{4,0},{8,12},{12,8},{16,20},{20,16},{24,28},{28,24},{1,5},{5... | collective-permute-start | bytes 1572872 | tf_op jit(solution)/shard_map/ppermute | solution.py:18
  21.8 7.2 %copy-start.3 = (pred[1024,1024]{1,0:T(8,128)(4,1)}, pred[1024,1024]{1,0:T(8,128)(4,1)S(1)}, u32[]{:S(2)}) copy-start(pred[1024,1024]{1,0:T(8,128)(4,1)S(1)} %iota_compare_fusion) | copy-start | bytes 3145732
  27.2 17.7 %copy-start.6 = (f32[4,8,1024]{2,1,0:T(8,128)S(1)}, f32[4,8,1024]{2,1,0:T(8,128)}, u32[]{:S(2)}) copy-start(f32[4,8,1024]{2,1,0:T(8,128)} %param.9) | copy-start | bytes 393220
  27.2 13.3 %collective-permute-start.1 = (f32[8,128,128]{2,1,0:T(8,128)S(1)}, f32[8,128,128]{2,1,0:T(8,128)}, u32[]{:S(2)}, u32[]{:S(2)}) collective-permute-start(f32[8,128,128]{2,1,0:T(8,128)S(1)} %get-tuple-element.28), channel_id=1, source_target_pairs={{0,8},{8,0},{4,12},{12,4},{16,24},{24,16},{20,28},{28,20},{1,9},{9... | collective-permute-start | bytes 1572872 | tf_op jit(solution)/shard_map/ppermute | solution.py:18
  42.4 24.7 %collective-permute-start.2 = (f32[8,128,128]{2,1,0:T(8,128)}, f32[8,128,128]{2,1,0:T(8,128)}, u32[]{:S(2)}, u32[]{:S(2)}) collective-permute-start(f32[8,128,128]{2,1,0:T(8,128)} %get-tuple-element.30), channel_id=1, source_target_pairs={{0,16},{16,0},{4,20},{20,4},{8,24},{24,8},{12,28},{28,12},{1,17},{... | collective-permute-start | bytes 1572872 | tf_op jit(solution)/shard_map/ppermute | solution.py:18
  78.5 17.7 %copy-start.7 = (f32[1024]{0:T(1024)S(1)}, f32[1024]{0:T(1024)}, u32[]{:S(2)}) copy-start(f32[1024]{0:T(1024)} %param.10) | copy-start | bytes 12292
  108.5 7.2 %slice-start = ((s8[12582912]{0:T(1024)(128)(4,1)}), s8[4194304]{0:T(1024)(128)(4,1)S(1)}, s32[]{:S(2)}) async-start(s8[12582912]{0:T(1024)(128)(4,1)} %bitcast.117), calls=%async_computation | async-start | bytes 8388608
  108.5 8.2 %slice-start.1 = ((s8[12582912]{0:T(1024)(128)(4,1)}), s8[4194304]{0:T(1024)(128)(4,1)S(1)}, s32[]{:S(2)}) async-start(s8[12582912]{0:T(1024)(128)(4,1)} %bitcast.117), calls=%async_computation.1 | async-start | bytes 8388608
  108.5 9.8 %slice-start.2 = ((s8[12582912]{0:T(1024)(128)(4,1)}), s8[4194304]{0:T(1024)(128)(4,1)S(1)}, s32[]{:S(2)}) async-start(s8[12582912]{0:T(1024)(128)(4,1)} %bitcast.117), calls=%async_computation.2 | async-start | bytes 8388608
  115.2 12.4 %copy-start.2 = (bf16[1024,8,128]{0,2,1:T(8,128)(2,1)}, bf16[1024,8,128]{0,2,1:T(8,128)(2,1)S(1)}, u32[]{:S(2)}) copy-start(bf16[1024,8,128]{0,2,1:T(8,128)(2,1)S(1)} %get-tuple-element.21) | copy-start | bytes 6291460
  118.3 5.1 %copy-start.1 = (bf16[128,8,8,128]{3,2,1,0:T(8,128)(2,1)S(1)}, bf16[128,8,8,128]{3,2,1,0:T(8,128)(2,1)}, u32[]{:S(2)}) copy-start(bf16[128,8,8,128]{3,2,1,0:T(8,128)(2,1)} %copy.74) | copy-start | bytes 6291460
  123.4 4.2 %copy-start.4 = (pred[1024,1024]{1,0:T(8,128)(4,1)S(1)}, pred[1024,1024]{1,0:T(8,128)(4,1)}, u32[]{:S(2)}) copy-start(pred[1024,1024]{1,0:T(8,128)(4,1)} %copy-done.3) | copy-start | bytes 3145732
  126.4 35.6 %collective-permute-start.3 = (f32[3,8,128,128]{2,3,0,1:T(8,128)}, f32[3,8,128,128]{2,3,0,1:T(8,128)}, u32[]{:S(2)}, u32[]{:S(2)}) collective-permute-start(f32[3,8,128,128]{2,3,0,1:T(8,128)} %multiply_bitcast_fusion), channel_id=1, source_target_pairs={{0,4},{4,0},{8,12},{12,8},{16,20},{20,16},{24,28},{28,24},{1,5},{5... | collective-permute-start | bytes 4718600 | tf_op jit(solution)/shard_map/ppermute | solution.py:18
  137.3 29.0 %slice-start.3 = ((s8[16777216]{0:T(1024)(128)(4,1)}), s8[4194304]{0:T(1024)(128)(4,1)S(1)}, s32[]{:S(2)}) async-start(s8[16777216]{0:T(1024)(128)(4,1)} %bitcast.119), calls=%async_computation.3 | async-start | bytes 8388608
  137.3 29.0 %slice-start.4 = ((s8[16777216]{0:T(1024)(128)(4,1)}), s8[4194304]{0:T(1024)(128)(4,1)S(1)}, s32[]{:S(2)}) async-start(s8[16777216]{0:T(1024)(128)(4,1)} %bitcast.119), calls=%async_computation.4 | async-start | bytes 8388608
  137.3 29.0 %slice-start.5 = ((s8[16777216]{0:T(1024)(128)(4,1)}), s8[4194304]{0:T(1024)(128)(4,1)S(1)}, s32[]{:S(2)}) async-start(s8[16777216]{0:T(1024)(128)(4,1)} %bitcast.119), calls=%async_computation.5 | async-start | bytes 8388608
  148.7 17.6 %slice-start.6 = ((s8[16777216]{0:T(1024)(128)(4,1)}), s8[4194304]{0:T(1024)(128)(4,1)S(1)}, s32[]{:S(2)}) async-start(s8[16777216]{0:T(1024)(128)(4,1)} %bitcast.119), calls=%async_computation.6 | async-start | bytes 8388608
  162.0 31.4 %slice-start.7 = ((s8[6291456]{0:T(1024)(128)(4,1)}), s8[4194304]{0:T(1024)(128)(4,1)S(1)}, s32[]{:S(2)}) async-start(s8[6291456]{0:T(1024)(128)(4,1)} %bitcast.125), calls=%async_computation.7 | async-start | bytes 8388608
  164.8 28.6 %slice-start.8 = ((s8[6291456]{0:T(1024)(128)(4,1)}), s8[2097152]{0:T(1024)(128)(4,1)S(1)}, s32[]{:S(2)}) async-start(s8[6291456]{0:T(1024)(128)(4,1)} %bitcast.125), calls=%async_computation.8 | async-start | bytes 4194304
  164.8 23.9 %collective-permute-start.4 = (f32[2,8,128,128]{2,3,0,1:T(8,128)}, f32[2,8,128,128]{2,3,0,1:T(8,128)}, u32[]{:S(2)}, u32[]{:S(2)}) collective-permute-start(f32[2,8,128,128]{2,3,0,1:T(8,128)} %slice_add_fusion), channel_id=1, source_target_pairs={{0,8},{8,0},{4,12},{12,4},{16,24},{24,16},{20,28},{28,20},{1,9},{9... | collective-permute-start | bytes 3145736 | tf_op jit(solution)/shard_map/ppermute | solution.py:18
  190.0 47.9 %collective-permute-start.5 = (f32[1,8,128,128]{2,3,0,1:T(8,128)S(1)}, f32[1,8,128,128]{2,3,0,1:T(8,128)}, u32[]{:S(2)}, u32[]{:S(2)}) collective-permute-start(f32[1,8,128,128]{2,3,0,1:T(8,128)S(1)} %slice_add_fusion.1), channel_id=1, source_target_pairs={{0,16},{16,0},{4,20},{20,4},{8,24},{24,8},{12,28},{28,12},{1,17},{... | collective-permute-start | bytes 1572872 | tf_op jit(solution)/shard_map/ppermute | solution.py:18
